TPU v7x, 32 devices: a whole 2x2x4 slice. The times are simulated.
32 devices in a mesh: st: 8 (over z, y), ob: 4 (over x, core).
Axes of the slice: x: 2, y: 2, z: 4, core: 2. Of those that a mesh axis runs over, the one named last changes fastest.
Arguments:
- ensemble: bfloat16 [18432, 64], P('st'), may hold values from -3 to 3
- weights: bfloat16 [4096, 64], P('ob'), may hold values from -6 to 6
- obs_column: int32 [4096], P('ob'), may hold values from 0 to 18431
Outputs:
- forecast: float32 [64, 3, 48, 128], P('ob', None, 'st')
All inputs are finite; a program needn't handle non-finite values.
Results may differ from a plain program's by a relative error of at most 0.0061.
Values may be sent and summed in bfloat16 or wider, within the bound.
A program may use at most 128 MiB of HBM per device.

v0:
```python
import jax
import jax.numpy as jnp
from jax import lax
from jax.sharding import PartitionSpec as P

NLON = 128
STEPS = 3
MEMBERS_PER_PART = 16


time_step = 0.3


def with_halo(block, sides, width):
    for axis, dim in sides:
        count = lax.axis_size(axis)
        forward = [(i, i + 1) for i in range(count - 1)]
        backward = [(target, source) for source, target in forward]
        low = lax.ppermute(
            lax.slice_in_dim(block, block.shape[dim] - width, None, axis=dim), axis, forward
        )
        high = lax.ppermute(lax.slice_in_dim(block, 0, width, axis=dim), axis, backward)
        block = jnp.concatenate([low, block, high], axis=dim)
    return block


def tapering(state_rows, columns, radius):
    state_lat = state_rows // (3 * NLON)
    state_lon = state_rows % NLON
    obs_lat = columns // (3 * NLON)
    obs_lon = columns % NLON
    lat_gap = state_lat[:, None] - obs_lat[None, :]
    lon_gap = jnp.abs(state_lon[:, None] - obs_lon[None, :])
    lon_gap = jnp.minimum(lon_gap, NLON - lon_gap)
    squared = (lat_gap * lat_gap + lon_gap * lon_gap).astype(jnp.float32)
    falloff = jnp.maximum(jnp.float32(0.0), 1.0 - squared / jnp.float32(radius * radius))
    return falloff * falloff


def advance(padded, latitude, lat_count):
    centre = padded[:, :, 1:-1]
    northern = padded[:, :, 2:]
    southern = padded[:, :, :-2]
    eastern = jnp.roll(centre, -1, axis=3)
    western = jnp.roll(centre, 1, axis=3)
    flux_east = (1.0 + padded[:, 0]) * padded[:, 1]
    flux_north = (1.0 + padded[:, 0]) * padded[:, 2]
    mid_east = flux_east[:, 1:-1]
    divergence = (jnp.roll(mid_east, -1, axis=2) - jnp.roll(mid_east, 1, axis=2)) / 2.0
    divergence = divergence + (flux_north[:, 2:] - flux_north[:, :-2]) / 2.0
    along_lon = (eastern - western) / 2.0
    along_lat = (northern - southern) / 2.0
    eastward = centre[:, 1]
    northward = centre[:, 2]
    coriolis = 0.8 * jnp.sin(jnp.pi * ((latitude.astype(jnp.float32) + 0.5) / lat_count - 0.5))
    coriolis = coriolis[None, :, None]
    tend_east = (
        eastward * along_lon[:, 1]
        + northward * along_lat[:, 1]
        + along_lon[:, 0]
        - coriolis * northward
    )
    tend_north = (
        eastward * along_lon[:, 2]
        + northward * along_lat[:, 2]
        + along_lat[:, 0]
        + coriolis * eastward
    )
    tendency = jnp.stack([divergence, tend_east, tend_north], axis=1)
    return 0.25 * (northern + southern + eastern + western) - time_step * tendency


def local(ensemble, weights, obs_column):
    row_count = ensemble.shape[0]
    members = ensemble.shape[1]
    lat_here = row_count // (3 * NLON)
    lat_count = lat_here * lax.axis_size("st")
    predicted_rows = ensemble.astype(jnp.float32)
    ensemble_mean = jnp.mean(predicted_rows, axis=1, keepdims=True)
    member_anomalies = (predicted_rows - ensemble_mean).astype(jnp.bfloat16)
    row_start = lax.axis_index("st") * row_count
    offset = obs_column - row_start
    inside_band = (offset >= 0) & (offset < row_count)
    clipped = jnp.clip(offset, 0, row_count - 1)
    picked = jnp.take(member_anomalies, clipped, axis=0)
    partial_value = jnp.where(inside_band[:, None], picked, jnp.zeros_like(picked)).astype(
        jnp.float32
    )
    obs_anom = lax.psum(partial_value.astype(jnp.bfloat16), "st")
    state_rows = row_start + jnp.arange(row_count, dtype=jnp.int32)
    covariance = lax.dot_general(
        member_anomalies, obs_anom, (((1,), (1,)), ((), ())), preferred_element_type=jnp.float32
    )
    kalman_gain = (
        covariance * tapering(state_rows, obs_column, lat_count) / jnp.float32(members - 1)
    ).astype(jnp.bfloat16)
    state_update = jnp.dot(kalman_gain, weights, preferred_element_type=jnp.float32)
    first_member = lax.axis_index("ob") * MEMBERS_PER_PART
    local_rows = lax.dynamic_slice_in_dim(predicted_rows, first_member, MEMBERS_PER_PART, 1)
    shared = lax.psum_scatter(state_update, "ob", scatter_dimension=1, tiled=True)
    updated_members = local_rows + shared
    fields = updated_members.reshape(lat_here, 3, NLON, MEMBERS_PER_PART).transpose(3, 1, 0, 2)
    band_start = lax.axis_index("st") * lat_here
    extended = with_halo(fields, (("st", 2),), STEPS)
    first_row = band_start - STEPS
    for section in range(STEPS):
        kept = extended.shape[2] - 2
        latitude = first_row + section + 1 + jnp.arange(kept, dtype=jnp.int32)
        extended = advance(extended, latitude, lat_count)
        inside = (latitude >= 0) & (latitude < lat_count)
        extended = jnp.where(inside[None, None, :, None], extended, jnp.float32(0.0))
    fields = extended
    return fields


def solution(mesh):
    return jax.shard_map(
        local,
        mesh=mesh,
        in_specs=(P("st", None), P("ob", None), P("ob")),
        out_specs=P("ob", None, "st", None),
        check_vma=False,
    )
```

profile of v0, /device:TPU:0, one launch (start us, length us, event | category | flops | bytes accessed | tf_op | source)
XLA Modules:
  0.0 137.9 jit_solution(10574656669796040680)
XLA Ops:
  6.5 0.7 add_select_fusion.3
  7.3 0.7 compare_and_fusion.1
  8.0 1.0 convert_reduce_fusion
  9.0 1.0 subtract_convert_fusion
  10.0 0.3 copy.60
  10.4 3.2 %gather_fusion = bf16[1024,64]{1,0:T(8,128)(2,1)S(1)} fusion(bf16[2304,64]{1,0:T(8,128)(2,1)S(1)} %copy.60, s32[1024]{0:T(1024)S(1)} %get-tuple-element.44), kind=kCustom, calls=%fused_computation | custom fusion | bytes 266240 | tf_op jit(solution)/shard_map/jit(_take)/gather | solution.py:85
  13.6 1.0 select_select_fusion
  14.7 73.8 %all-reduce.2.cloned.1.call-done = bf16[1024,64]{1,0:T(8,128)(2,1)} async-done(((bf16[1024,64]{1,0:T(8,128)(2,1)}), bf16[1024,64]{1,0:T(8,128)(2,1)}) %all-reduce.2.cloned.1.call-update) | async-done | bytes 131088 | tf_op jit(solution)/shard_map/psum | solution.py:89
  88.5 8.5 %fusion.10 = f32[2304,64]{0,1:T(8,128)} fusion(bf16[1024,64]{0,1:T(8,128)(2,1)S(1)} %copy-done, bf16[2304,64]{0,1:T(8,128)(2,1)S(1)} %subtract_convert_fusion, bf16[1024,64]{1,0:T(8,128)(2,1)} %all-reduce.2.cloned.1.call-done, s32[1024]{0:T(1024)S(1)} %get-tuple-element.45, s32[2304]{0:T(1024)S(1)} %get-tuple-element.48, s32[1024]{0:T(1024)S(1)} %get-tuple-element.43, ...), kind=kOutput, calls=%fused_computation.12 | convolution fusion | flops 641728512 | bytes 1173504 | tf_op jit(solution)/shard_map/dot_general | solution.py:97
  97.0 0.9 copy-done.1
  98.2 20.2 %reduce-scatter.2.cloned.1.call-done = f32[2304,16]{0,1:T(8,128)} async-done(((f32[2304,64]{0,1:T(8,128)}), f32[2304,16]{0,1:T(8,128)}) %reduce-scatter.2.cloned.1.call-update) | async-done | bytes 147472 | tf_op jit(solution)/shard_map/reduce_scatter | solution.py:100
  118.4 0.9 dynamic-slice_add_fusion
  119.5 1.3 collective-permute-start.1
  120.8 4.5 %collective-permute-start = (f32[16,3,3,128]{3,0,2,1:T(8,128)S(1)}, f32[16,3,3,128]{3,0,2,1:T(8,128)S(1)}, u32[]{:S(2)}, u32[]{:S(2)}) collective-permute-start(f32[16,3,3,128]{3,0,2,1:T(8,128)S(1)} %get-tuple-element.29), channel_id=1, source_target_pairs={{0,4},{4,8},{8,12},{12,16},{16,20},{20,24},{24,28},{1,5},{5,9},{9,... | collective-permute-start | bytes 221192 | tf_op jit(solution)/shard_map/ppermute | solution.py:19
  125.4 0.4 collective-permute-done.1
  125.7 1.6 %collective-permute-done = f32[16,3,3,128]{3,0,2,1:T(8,128)S(1)} collective-permute-done((f32[16,3,3,128]{3,0,2,1:T(8,128)S(1)}, f32[16,3,3,128]{3,0,2,1:T(8,128)S(1)}, u32[]{:S(2)}, u32[]{:S(2)}) %collective-permute-start) | collective-permute-done | bytes 73760 | tf_op jit(solution)/shard_map/ppermute | solution.py:19
  127.3 0.1 fusion.57
  127.5 0.1 fusion.58
  127.8 0.2 subtract_multiply_fusion.1
  128.3 0.2 fusion.12
  128.9 0.2 subtract_multiply_fusion.3
  129.3 0.2 fusion.14
  129.9 0.2 subtract_multiply_fusion.5
  130.3 0.8 fusion.16
  (42 shorter events, 2.1 us)
Async XLA Ops:
  6.5 82.0 %copy-start = (bf16[1024,64]{0,1:T(8,128)(2,1)S(1)}, bf16[1024,64]{0,1:T(8,128)(2,1)}, u32[]{:S(2)}) copy-start(bf16[1024,64]{0,1:T(8,128)(2,1)} %param.4) | copy-start | bytes 393220
  6.5 82.0 %all-reduce.2.cloned.1.call-start = ((), (), s32[]{:S(2)}) async-start(), calls=%async_computation.1 | async-start | bytes 524288 | tf_op jit(solution)/shard_map/psum | solution.py:89
  14.6 103.8 %reduce-scatter.2.cloned.1.call-start = ((), (), s32[]{:S(2)}) async-start(), calls=%async_computation.2 | async-start | bytes 737280 | tf_op jit(solution)/shard_map/reduce_scatter | solution.py:100
  97.0 1.0 copy-start.1
  119.5 6.2 %collective-permute-start.1 = (f32[16,3,3,128]{3,0,2,1:T(8,128)S(1)}, f32[16,3,3,128]{3,0,2,1:T(8,128)S(1)}, u32[]{:S(2)}, u32[]{:S(2)}) collective-permute-start(f32[16,3,3,128]{3,0,2,1:T(8,128)S(1)} %get-tuple-element.30), channel_id=1, source_target_pairs={{4,0},{8,4},{12,8},{16,12},{20,16},{24,20},{28,24},{5,1},{9,5},{13... | collective-permute-start | bytes 221192 | tf_op jit(solution)/shard_map/ppermute | solution.py:22
  120.8 6.5 %collective-permute-start = (f32[16,3,3,128]{3,0,2,1:T(8,128)S(1)}, f32[16,3,3,128]{3,0,2,1:T(8,128)S(1)}, u32[]{:S(2)}, u32[]{:S(2)}) collective-permute-start(f32[16,3,3,128]{3,0,2,1:T(8,128)S(1)} %get-tuple-element.29), channel_id=1, source_target_pairs={{0,4},{4,8},{8,12},{12,16},{16,20},{20,24},{24,28},{1,5},{5,9},{9,... | collective-permute-start | bytes 221192 | tf_op jit(solution)/shard_map/ppermute | solution.py:19
Sparse Core Ops, SparseCore 0:
  14.8 73.7 all-reduce.1
  97.2 21.2 reduce-scatter.1
where the time goes:
time: 139 us; the launch traced here: 138 us
  waiting for transfers between devices  96 us (69%)
  between operations  13.7 us (10%)
  matrix products  8.51 us (6%)
  other arithmetic  8.14 us (6%)
  starting transfers between devices  5.89 us (4%)
  local copies, waits for them, and re-layouts  5.74 us (4%)
    psum x1, waiting for transfers between devices, local(): obs_anom = lax.psum(partial_value.astype(jnp.bfloat16), 'st')  73.8 us
    reduce_scatter x1, waiting for transfers between devices, local(): lax.psum_scatter(state_update, 'ob', scatter_dimension=1, tiled=True)  20.2 us
    dot_general x1, matrix products, local(): jnp.dot(kalman_gain, weights, preferred_element_type=jnp.float32)  8.51 us
    ppermute x1, starting transfers between devices, with_halo(): lax.ppermute(lax.slice_in_dim(block, block.shape[dim] - width, None, axis...  4.55 us
    gather x1, local copies, waits for them, and re-layouts, local(): picked = jnp.take(member_anomalies, clipped, axis=0)  3.21 us
  transfers between devices with their start and end apart: 4, of which 4 were waited for; matrix products, arithmetic and copies ran while one was open for 0% of the time, Pallas kernels for 0%

commit v1 on v0

v1 whole, which is shorter than its diff:
```python
import functools

import jax
import jax.numpy as jnp
import numpy as np
from jax import lax
from jax.experimental import pallas as pl
from jax.experimental.pallas import tpu as pltpu
from jax.sharding import PartitionSpec as P

NLON = 128
FIELDS = 3
STEPS = 3
MESH = pl.DeviceIdType.MESH
time_step = 0.3
F32 = jnp.float32
BF16 = jnp.bfloat16


def remote(src, dst, send, recv, device):
    return pltpu.make_async_remote_copy(
        src_ref=src, dst_ref=dst, send_sem=send, recv_sem=recv, device_id=device, device_id_type=MESH
    )


def analysis_kernel(
    n_st, n_ob, ens_ref, w_ref, col_ref, out_ref,
    anom_t, anom, own, picked, part, gathered, obs_t, taper, inc, inc_send, inc_recv,
    p_send, p_recv, g_send, g_recv, i_send, i_recv, h_send, h_recv,
):
    st, ob = lax.axis_index("st"), lax.axis_index("ob")
    rows, members = ens_ref.shape
    obs = w_ref.shape[0]
    per = members // n_ob
    lats = rows // (FIELDS * NLON)
    blocks = rows // NLON
    chunk = obs // n_st
    radius2 = float((lats * n_st) ** 2)

    barrier = pltpu.get_barrier_semaphore()
    for d in range(1, n_st):
        pl.semaphore_signal(barrier, inc=1, device_id={"st": lax.rem(st + d, n_st)}, device_id_type=MESH)
    for d in range(1, n_ob):
        pl.semaphore_signal(barrier, inc=1, device_id={"ob": lax.rem(ob + d, n_ob)}, device_id_type=MESH)

    for b in range(blocks):
        e_t = ens_ref[b * NLON:(b + 1) * NLON, :].astype(F32).T
        mean = jnp.sum(e_t, axis=0, keepdims=True) / members
        anom_t[:, b * NLON:(b + 1) * NLON] = (e_t - mean).astype(BF16)
        own[:, b] = e_t.reshape(n_ob, per, NLON)

    column = col_ref[...]
    depth = 2 * FIELDS * NLON if lats % 2 == 0 else FIELDS * NLON
    relative = column - st * rows
    spot = lax.broadcasted_iota(jnp.int32, (depth, obs), 0)
    total = jnp.zeros((members, obs), F32)
    for k in range(rows // depth):
        hot = jnp.where(spot == relative - k * depth, F32(1.0), F32(0.0)).astype(BF16)
        total = total + jnp.dot(anom_t[:, k * depth:(k + 1) * depth], hot, preferred_element_type=F32)
    total = total.astype(BF16)
    for c in range(n_st):
        picked[c] = total[:, c * chunk:(c + 1) * chunk]

    pl.semaphore_wait(barrier, n_st - 1 + n_ob - 1)

    first = []
    for d in range(1, n_st):
        peer = lax.rem(st + d, n_st)
        first.append(remote(picked.at[peer], part.at[d], p_send.at[d], p_recv.at[d], {"st": peer}))
    for copy in first:
        copy.start()

    ones = jnp.ones((members, members), BF16)
    for l in range(lats):
        band = slice(l * FIELDS * NLON, (l + 1) * FIELDS * NLON)
        e = ens_ref[band, :]
        mean = jnp.dot(e, ones, preferred_element_type=F32) / members
        anom[l] = (e.astype(F32) - mean).astype(BF16)
    obs_lat = jnp.floor((column.astype(F32) + 0.5) * (1.0 / (FIELDS * NLON)))
    obs_lon = (column & (NLON - 1)).astype(F32)
    lon = lax.broadcasted_iota(jnp.int32, (NLON, obs), 0).astype(F32)
    lon_gap = jnp.abs(lon - obs_lon)
    lon_gap = jnp.minimum(lon_gap, NLON - lon_gap)
    lon_left = radius2 - lon_gap * lon_gap
    scale = 1.0 / (radius2 * radius2 * (members - 1))
    for l in range(lats):
        lat_gap = obs_lat - (st * lats + l).astype(F32)
        fall = jnp.maximum(lon_left - lat_gap * lat_gap, 0.0)
        taper[l] = fall * (fall * scale)

    for copy in first:
        copy.wait_recv()
    mine = picked[st].astype(F32)
    for d in range(1, n_st):
        mine = mine + part[d].astype(F32)
    gathered[st] = mine.astype(BF16)

    second = []
    for d in range(1, n_st):
        peer = lax.rem(st + d, n_st)
        second.append(remote(gathered.at[st], gathered.at[st], g_send.at[d], g_recv.at[d], {"st": peer}))
    for copy in second:
        copy.start()
    for copy in second:
        copy.wait_recv()
    for c in range(n_st):
        obs_t[:, c * chunk:(c + 1) * chunk] = gathered[c]

    width = min(256, obs)

    def sends(l):
        return [
            remote(
                inc_send.at[lax.rem(ob + d, n_ob), l], inc_recv.at[d, l],
                i_send.at[d, l], i_recv.at[d, l], {"ob": lax.rem(ob + d, n_ob)},
            )
            for d in range(1, n_ob)
        ]

    def latitude(l, carry):
        total = jnp.zeros((FIELDS * NLON, members), F32)
        a = anom[l]
        for k in range(obs // width):
            at = slice(k * width, (k + 1) * width)
            cov = jnp.dot(a, obs_t[:, at], preferred_element_type=F32)
            gain = cov.reshape(FIELDS, NLON, width) * taper[l, :, at][None]
            gain = gain.astype(BF16).reshape(FIELDS * NLON, width)
            total = total + jnp.dot(gain, w_ref[at, :], preferred_element_type=F32)
        for f in range(FIELDS):
            turned = total[f * NLON:(f + 1) * NLON, :].T.reshape(n_ob, per, NLON)
            inc[:, l, f] = turned
            inc_send[:, l, f] = turned.astype(BF16)
        for copy in sends(l):
            copy.start()
        return carry

    lax.fori_loop(0, lats, latitude, 0)

    for l in range(lats):
        for copy in sends(l):
            copy.wait_recv()
        for f in range(FIELDS):
            value = own[ob, l * FIELDS + f] + inc[ob, l, f]
            for d in range(1, n_ob):
                value = value + inc_recv[d, l, f].astype(F32)
            out_ref[STEPS + l, f] = value

    up = remote(
        out_ref.at[pl.ds(lats, STEPS)], out_ref.at[pl.ds(0, STEPS)],
        h_send.at[0], h_recv.at[0], {"st": lax.rem(st + 1, n_st)},
    )
    down = remote(
        out_ref.at[pl.ds(STEPS, STEPS)], out_ref.at[pl.ds(STEPS + lats, STEPS)],
        h_send.at[1], h_recv.at[1], {"st": lax.rem(st + n_st - 1, n_st)},
    )

    @pl.when(st < n_st - 1)
    def _():
        up.start()

    @pl.when(st > 0)
    def _():
        down.start()

    @pl.when(st == 0)
    def _():
        out_ref[0:STEPS] = jnp.zeros((STEPS,) + out_ref.shape[1:], F32)

    @pl.when(st == n_st - 1)
    def _():
        out_ref[STEPS + lats:] = jnp.zeros((STEPS,) + out_ref.shape[1:], F32)

    for copy in first + second:
        copy.wait_send()
    for l in range(lats):
        for copy in sends(l):
            copy.wait_send()

    @pl.when(st < n_st - 1)
    def _():
        up.wait_send()
        down.wait_recv()

    @pl.when(st > 0)
    def _():
        down.wait_send()
        up.wait_recv()


def forecast_kernel(n_st, coriolis_ref, ext_ref, out_ref):
    st = lax.axis_index("st")
    lats = ext_ref.shape[0] - 2 * STEPS
    lat_count = lats * n_st

    def east(q):
        return pltpu.roll(q, NLON - 1, 2)

    def west(q):
        return pltpu.roll(q, 1, 2)

    h, u, v = (ext_ref[:, f] for f in range(FIELDS))
    for step in range(STEPS):
        flux_east = (1.0 + h[1:-1]) * u[1:-1]
        flux_north = (1.0 + h) * v
        around, dlon, dlat = [], [], []
        for q in (h, u, v):
            c = q[1:-1]
            e, w, n, s = east(c), west(c), q[2:], q[:-2]
            around.append(0.25 * (n + s + e + w))
            dlon.append((e - w) * 0.5)
            dlat.append((n - s) * 0.5)
        divergence = (east(flux_east) - west(flux_east)) * 0.5 + (flux_north[2:] - flux_north[:-2]) * 0.5
        cu, cv = u[1:-1], v[1:-1]
        count = cu.shape[0]
        base = st * lats - STEPS + step + 1
        new = [[], [], []]
        for i in range(count):
            latitude = base + i
            inside = (latitude >= 0) & (latitude < lat_count)
            keep = jnp.where(inside, F32(1.0), F32(0.0))
            turn = coriolis_ref[0, jnp.clip(latitude, 0, lat_count - 1)]
            tend_u = cu[i] * dlon[1][i] + cv[i] * dlat[1][i] + dlon[0][i] - turn * cv[i]
            tend_v = cu[i] * dlon[2][i] + cv[i] * dlat[2][i] + dlat[0][i] + turn * cu[i]
            for f, tend in enumerate((divergence[i], tend_u, tend_v)):
                value = around[f][i] - time_step * tend
                if step < STEPS - 1:
                    new[f].append(jnp.where(keep > 0.5, value, 0.0))
                else:
                    out_ref[:, f, i, :] = value
        if step < STEPS - 1:
            h, u, v = (jnp.stack(q) for q in new)


def local(n_st, n_ob, ensemble, weights, obs_column):
    rows, members = ensemble.shape
    obs = weights.shape[0]
    per = members // n_ob
    lats = rows // (FIELDS * NLON)
    blocks = rows // NLON
    chunk = obs // n_st
    vmem = pl.BlockSpec(memory_space=pltpu.VMEM)
    dma = pltpu.SemaphoreType.DMA
    ext = pl.pallas_call(
        functools.partial(analysis_kernel, n_st, n_ob),
        out_shape=jax.ShapeDtypeStruct((lats + 2 * STEPS, FIELDS, per, NLON), F32),
        in_specs=[vmem] * 3,
        out_specs=vmem,
        scratch_shapes=[
            pltpu.VMEM((members, rows), BF16),
            pltpu.VMEM((lats, FIELDS * NLON, members), BF16),
            pltpu.VMEM((n_ob, blocks, per, NLON), F32),
            pltpu.VMEM((n_st, members, chunk), BF16),
            pltpu.VMEM((n_st, members, chunk), BF16),
            pltpu.VMEM((n_st, members, chunk), BF16),
            pltpu.VMEM((members, obs), BF16),
            pltpu.VMEM((lats, NLON, obs), F32),
            pltpu.VMEM((n_ob, lats, FIELDS, per, NLON), F32),
            pltpu.VMEM((n_ob, lats, FIELDS, per, NLON), BF16),
            pltpu.VMEM((n_ob, lats, FIELDS, per, NLON), BF16),
            dma((n_st,)), dma((n_st,)), dma((n_st,)), dma((n_st,)),
            dma((n_ob, lats)), dma((n_ob, lats)), dma((2,)), dma((2,)),
        ],
        compiler_params=pltpu.CompilerParams(
            collective_id=0, has_side_effects=True, vmem_limit_bytes=48 * 1024 * 1024
        ),
        name="analysis",
    )(ensemble, weights, obs_column.reshape(1, obs))
    lat_count = lats * n_st
    degrees = (np.arange(lat_count, dtype=np.float32) + 0.5) / lat_count - 0.5
    coriolis = (0.8 * np.sin(np.pi * degrees)).astype(np.float32).reshape(1, lat_count)
    return pl.pallas_call(
        functools.partial(forecast_kernel, n_st),
        out_shape=jax.ShapeDtypeStruct((per, FIELDS, lats, NLON), F32),
        in_specs=[pl.BlockSpec(memory_space=pltpu.SMEM), vmem],
        out_specs=vmem,
        name="forecast",
    )(jnp.asarray(coriolis), ext)


def solution(mesh):
    return jax.shard_map(
        functools.partial(local, mesh.shape["st"], mesh.shape["ob"]),
        mesh=mesh,
        in_specs=(P("st", None), P("ob", None), P("ob")),
        out_specs=P("ob", None, "st", None),
        check_vma=False,
    )
```

time: 139 us -> 34.1 us (0.25)
  waiting for transfers between devices: 96 us -> 0 us
  Pallas kernels: 0 us -> 29.7 us
  between operations: 13.7 us -> 0.05 us
  matrix products: 8.51 us -> 0 us
  other arithmetic: 8.14 us -> 0 us
  starting transfers between devices: 5.89 us -> 0 us
  local copies, waits for them, and re-layouts: 5.74 us -> 4.1 us
    psum x1 -> x0, waiting for transfers between devices: 73.8 us -> none  [local(): obs_anom = lax.psum(partial_value.astype(jnp.bfloat16), 'st')]
    pallas_call x0 -> x2, Pallas kernels: none -> 29.7 us  [the longest x1 27.4 us: local(): pl.pallas_call(functools.partial(analysis_kernel, n_st, n_ob), out_shape=...]
    reduce_scatter x1 -> x0, waiting for transfers between devices: 20.2 us -> none  [local(): lax.psum_scatter(state_update, 'ob', scatter_dimension=1, tiled=True)]
    dot_general x1 -> x0, matrix products: 8.51 us -> none  [local(): jnp.dot(kalman_gain, weights, preferred_element_type=jnp.float32)]
    ppermute x2 -> x0, starting transfers between devices: 5.84 us -> none  [the longest x1 4.55 us: with_halo(): lax.ppermute(lax.slice_in_dim(block, block.shape[dim] - width, None, axis...]
    gather x1 -> x0, local copies, waits for them, and re-layouts: 3.21 us -> none  [local(): picked = jnp.take(member_anomalies, clipped, axis=0)]
    select_n x6 -> x0, other arithmetic: 3.01 us -> none  [the longest x3 1.22 us: local(): jnp.where(inside[None, None, :, None], extended, jnp.float32(0.0))]
    ppermute x2 -> x0, waiting for transfers between devices: 1.95 us -> none  [the longest x1 1.57 us: with_halo(): lax.ppermute(lax.slice_in_dim(block, block.shape[dim] - width, None, axis...]
  transfers between devices with their start and end apart: 4 -> 0, of which waited for: 4 -> 0; matrix products, arithmetic and copies ran while one was open for 0% -> 0% of each run, Pallas kernels for 0% -> 0%
where the time goes in v1:
time: 34.1 us; the launch traced here: 33.9 us
  Pallas kernels  29.7 us (87%)
  local copies, waits for them, and re-layouts  4.1 us (12%)
    pallas_call x1, Pallas kernels, local(): pl.pallas_call(functools.partial(analysis_kernel, n_st, n_ob), out_shape=...  27.4 us
    unnamed x8, local copies, waits for them, and re-layouts  2.49 us
    pallas_call x1, Pallas kernels, local(): pl.pallas_call(functools.partial(forecast_kernel, n_st), out_shape=jax.Sh...  2.34 us
    pallas_call x1, local copies, waits for them, and re-layouts, local(): pl.pallas_call(functools.partial(forecast_kernel, n_st), out_shape=jax.Sh...  1.61 us

profile of v1, /device:TPU:0, one launch (start us, length us, event | category | flops | bytes accessed | tf_op | source)
XLA Modules:
  0.0 33.9 jit_solution(3764834965275165484)
XLA Ops:
  0.0 0.0 copy-start.2
  0.0 1.1 %copy.6.w_ref = bf16[1024,64]{1,0:T(8,128)(2,1)S(1)} copy(bf16[1024,64]{0,1:T(8,128)(2,1)} %param.5) | data formatting | bytes 262144 | tf_op args[1]
  1.1 0.0 copy-done.2
  1.1 0.0 copy-start.1
  1.1 0.3 copy.5.ens_ref
  1.5 0.4 %copy-done.1 = s32[1024]{0:T(1024)S(1)} copy-done((s32[1024]{0:T(1024)S(1)}, s32[1024]{0:T(1024)}, u32[]{:S(2)}) %copy-start.1) | copy-done | bytes 4120
  1.8 27.4 %analysis.1.ext_ref = f32[12,3,16,128]{3,2,1,0:T(8,128)S(1)} custom-call(bf16[2304,64]{1,0:T(8,128)(2,1)S(1)} %copy.5.ens_ref, bf16[1024,64]{1,0:T(8,128)(2,1)S(1)} %copy.6.w_ref, s32[1,1024]{1,0:T(1,128)S(1)} %bitcast.1), custom_call_target="tpu_custom_call" | custom-call | tf_op jit(solution)/shard_map/analysis/pallas_call | solution.py:243
  29.2 0.0 copy-start
  29.2 0.7 %copy-done = f32[12,3,16,128]{3,2,1,0:T(8,128)} copy-done((f32[12,3,16,128]{3,2,1,0:T(8,128)}, f32[12,3,16,128]{3,2,1,0:T(8,128)S(1)}, u32[]{:S(2)}) %copy-start) | copy-done | bytes 294936
  29.9 2.3 %forecast.1 = f32[16,3,6,128]{3,2,1,0:T(8,128)} custom-call(f32[1,48]{1,0:T(1,128)} %constant.2.clone.coriolis_ref, f32[12,3,16,128]{3,2,1,0:T(8,128)} %copy-done), custom_call_target="tpu_custom_call" | custom-call | tf_op jit(solution)/shard_map/forecast/pallas_call | solution.py:271
  32.3 1.6 %copy.7 = f32[16,3,6,128]{3,0,2,1:T(8,128)} copy(f32[16,3,6,128]{3,2,1,0:T(8,128)} %forecast.1) | data formatting | bytes 294912 | tf_op jit(solution)/shard_map/forecast/pallas_call | solution.py:271
Async XLA Ops:
  0.0 1.1 %copy-start.2 = (bf16[2304,64]{0,1:T(8,128)(2,1)S(1)}, bf16[2304,64]{0,1:T(8,128)(2,1)}, u32[]{:S(2)}) copy-start(bf16[2304,64]{0,1:T(8,128)(2,1)} %param.4) | copy-start | bytes 884740
  1.1 0.7 %copy-start.1 = (s32[1024]{0:T(1024)S(1)}, s32[1024]{0:T(1024)}, u32[]{:S(2)}) copy-start(s32[1024]{0:T(1024)} %param.6) | copy-start | bytes 12292
  29.2 0.7 %copy-start = (f32[12,3,16,128]{3,2,1,0:T(8,128)}, f32[12,3,16,128]{3,2,1,0:T(8,128)S(1)}, u32[]{:S(2)}) copy-start(f32[12,3,16,128]{3,2,1,0:T(8,128)S(1)} %analysis.1.ext_ref) | copy-start | bytes 884740

commit v2 on v1

--- a/solution.py
+++ b/solution.py
@@ -24,31 +24,38 @@
 
 
 def analysis_kernel(
-    n_st, n_ob, ens_ref, w_ref, col_ref, out_ref,
-    anom_t, anom, own, picked, part, gathered, obs_t, taper, inc, inc_send, inc_recv,
+    n_st, n_ob, ens_hbm, w_hbm, col_hbm, out_ref, ens_ref, w_ref, col_ref, loaded,
+    anom_t, anom, w, picked, part, gathered, obs_t, taper, inc, inc_send, inc_recv,
     p_send, p_recv, g_send, g_recv, i_send, i_recv, h_send, h_recv,
 ):
     st, ob = lax.axis_index("st"), lax.axis_index("ob")
-    rows, members = ens_ref.shape
-    obs = w_ref.shape[0]
+    members, rows = ens_ref.shape
+    obs = w_ref.shape[1]
     per = members // n_ob
     lats = rows // (FIELDS * NLON)
     blocks = rows // NLON
     chunk = obs // n_st
     radius2 = float((lats * n_st) ** 2)
 
+    loads = [
+        pltpu.make_async_copy(src, dst, loaded.at[i])
+        for i, (src, dst) in enumerate(((ens_hbm, ens_ref), (col_hbm, col_ref), (w_hbm, w_ref)))
+    ]
+    for load in loads:
+        load.start()
     barrier = pltpu.get_barrier_semaphore()
     for d in range(1, n_st):
         pl.semaphore_signal(barrier, inc=1, device_id={"st": lax.rem(st + d, n_st)}, device_id_type=MESH)
     for d in range(1, n_ob):
         pl.semaphore_signal(barrier, inc=1, device_id={"ob": lax.rem(ob + d, n_ob)}, device_id_type=MESH)
 
+    loads[0].wait()
     for b in range(blocks):
-        e_t = ens_ref[b * NLON:(b + 1) * NLON, :].astype(F32).T
+        e_t = ens_ref[:, b * NLON:(b + 1) * NLON].astype(F32)
         mean = jnp.sum(e_t, axis=0, keepdims=True) / members
         anom_t[:, b * NLON:(b + 1) * NLON] = (e_t - mean).astype(BF16)
-        own[:, b] = e_t.reshape(n_ob, per, NLON)
-
+
+    loads[1].wait()
     column = col_ref[...]
     depth = 2 * FIELDS * NLON if lats % 2 == 0 else FIELDS * NLON
     relative = column - st * rows
@@ -70,12 +77,14 @@
     for copy in first:
         copy.start()
 
-    ones = jnp.ones((members, members), BF16)
-    for l in range(lats):
-        band = slice(l * FIELDS * NLON, (l + 1) * FIELDS * NLON)
-        e = ens_ref[band, :]
-        mean = jnp.dot(e, ones, preferred_element_type=F32) / members
-        anom[l] = (e.astype(F32) - mean).astype(BF16)
+    for b in range(blocks):
+        l, f = divmod(b, FIELDS)
+        block = anom_t[:, b * NLON:(b + 1) * NLON].astype(F32)
+        anom[l, f * NLON:(f + 1) * NLON, :] = block.T.astype(BF16)
+    loads[2].wait()
+    for b in range(obs // NLON):
+        at = slice(b * NLON, (b + 1) * NLON)
+        w[at, :] = w_ref[:, at].astype(F32).T.astype(BF16)
     obs_lat = jnp.floor((column.astype(F32) + 0.5) * (1.0 / (FIELDS * NLON)))
     obs_lon = (column & (NLON - 1)).astype(F32)
     lon = lax.broadcasted_iota(jnp.int32, (NLON, obs), 0).astype(F32)
@@ -125,7 +134,7 @@
             cov = jnp.dot(a, obs_t[:, at], preferred_element_type=F32)
             gain = cov.reshape(FIELDS, NLON, width) * taper[l, :, at][None]
             gain = gain.astype(BF16).reshape(FIELDS * NLON, width)
-            total = total + jnp.dot(gain, w_ref[at, :], preferred_element_type=F32)
+            total = total + jnp.dot(gain, w[at, :], preferred_element_type=F32)
         for f in range(FIELDS):
             turned = total[f * NLON:(f + 1) * NLON, :].T.reshape(n_ob, per, NLON)
             inc[:, l, f] = turned
@@ -136,11 +145,12 @@
 
     lax.fori_loop(0, lats, latitude, 0)
 
+    own = ens_ref[pl.ds(pl.multiple_of(ob * per, per), per), :].astype(F32)
     for l in range(lats):
         for copy in sends(l):
             copy.wait_recv()
         for f in range(FIELDS):
-            value = own[ob, l * FIELDS + f] + inc[ob, l, f]
+            value = own[:, (l * FIELDS + f) * NLON:(l * FIELDS + f + 1) * NLON] + inc[ob, l, f]
             for d in range(1, n_ob):
                 value = value + inc_recv[d, l, f].astype(F32)
             out_ref[STEPS + l, f] = value
@@ -226,7 +236,7 @@
                 if step < STEPS - 1:
                     new[f].append(jnp.where(keep > 0.5, value, 0.0))
                 else:
-                    out_ref[:, f, i, :] = value
+                    out_ref[f, i] = value
         if step < STEPS - 1:
             h, u, v = (jnp.stack(q) for q in new)
 
@@ -236,19 +246,22 @@
     obs = weights.shape[0]
     per = members // n_ob
     lats = rows // (FIELDS * NLON)
-    blocks = rows // NLON
     chunk = obs // n_st
     vmem = pl.BlockSpec(memory_space=pltpu.VMEM)
     dma = pltpu.SemaphoreType.DMA
     ext = pl.pallas_call(
         functools.partial(analysis_kernel, n_st, n_ob),
         out_shape=jax.ShapeDtypeStruct((lats + 2 * STEPS, FIELDS, per, NLON), F32),
-        in_specs=[vmem] * 3,
+        in_specs=[pl.BlockSpec(memory_space=pltpu.HBM)] * 3,
         out_specs=vmem,
         scratch_shapes=[
             pltpu.VMEM((members, rows), BF16),
+            pltpu.VMEM((members, obs), BF16),
+            pltpu.VMEM((1, obs), jnp.int32),
+            dma((3,)),
+            pltpu.VMEM((members, rows), BF16),
             pltpu.VMEM((lats, FIELDS * NLON, members), BF16),
-            pltpu.VMEM((n_ob, blocks, per, NLON), F32),
+            pltpu.VMEM((obs, members), BF16),
             pltpu.VMEM((n_st, members, chunk), BF16),
             pltpu.VMEM((n_st, members, chunk), BF16),
             pltpu.VMEM((n_st, members, chunk), BF16),
@@ -264,17 +277,19 @@
             collective_id=0, has_side_effects=True, vmem_limit_bytes=48 * 1024 * 1024
         ),
         name="analysis",
-    )(ensemble, weights, obs_column.reshape(1, obs))
+    )(ensemble.T, weights.T, obs_column.reshape(1, obs))
     lat_count = lats * n_st
     degrees = (np.arange(lat_count, dtype=np.float32) + 0.5) / lat_count - 0.5
     coriolis = (0.8 * np.sin(np.pi * degrees)).astype(np.float32).reshape(1, lat_count)
-    return pl.pallas_call(
+    fields = pl.pallas_call(
         functools.partial(forecast_kernel, n_st),
-        out_shape=jax.ShapeDtypeStruct((per, FIELDS, lats, NLON), F32),
+        out_shape=jax.ShapeDtypeStruct((FIELDS, lats, per, NLON), F32),
         in_specs=[pl.BlockSpec(memory_space=pltpu.SMEM), vmem],
         out_specs=vmem,
+        compiler_params=pltpu.CompilerParams(vmem_limit_bytes=8 * 1024 * 1024),
         name="forecast",
     )(jnp.asarray(coriolis), ext)
+    return fields.transpose(2, 0, 1, 3)
 
 
 def solution(mesh):

time: 34.1 us -> 32.3 us (0.947)
  local copies, waits for them, and re-layouts: 4.1 us -> 2.55 us
    pallas_call x1 -> x0, local copies, waits for them, and re-layouts: 1.61 us -> none  [local(): pl.pallas_call(functools.partial(forecast_kernel, n_st), out_shape=jax.Sh...]
    pallas_call x1, Pallas kernels: 2.34 us -> 1.84 us  [local(): pl.pallas_call(functools.partial(forecast_kernel, n_st), out_shape=jax.Sh...]
where the time goes in v2:
time: 32.3 us; the launch traced here: 32.1 us
  Pallas kernels  29.5 us (91%)
  local copies, waits for them, and re-layouts  2.55 us (8%)
    pallas_call x1, Pallas kernels, local(): pl.pallas_call(functools.partial(analysis_kernel, n_st, n_ob), out_shape=...  27.7 us
    unnamed x8, local copies, waits for them, and re-layouts  2.55 us
    pallas_call x1, Pallas kernels, local(): pl.pallas_call(functools.partial(forecast_kernel, n_st), out_shape=jax.Sh...  1.84 us

profile of v2, /device:TPU:0, one launch (start us, length us, event | category | flops | bytes accessed | tf_op | source)
XLA Modules:
  0.0 32.1 jit_solution(18057802693557768851)
XLA Ops:
  0.0 0.0 copy-start.2
  0.0 0.7 %copy-done.2 = s32[1024]{0:T(1024)S(1)} copy-done((s32[1024]{0:T(1024)S(1)}, s32[1024]{0:T(1024)}, u32[]{:S(2)}) %copy-start.2) | copy-done | bytes 4120
  0.7 0.0 copy-start
  0.7 1.0 %copy-done = bf16[2304,64]{0,1:T(8,128)(2,1)S(1)} copy-done((bf16[2304,64]{0,1:T(8,128)(2,1)S(1)}, bf16[2304,64]{0,1:T(8,128)(2,1)}, u32[]{:S(2)}) %copy-start) | copy-done | bytes 294936
  1.6 0.0 copy-start.1
  1.7 0.9 %copy-done.1 = bf16[1024,64]{0,1:T(8,128)(2,1)S(1)} copy-done((bf16[1024,64]{0,1:T(8,128)(2,1)S(1)}, bf16[1024,64]{0,1:T(8,128)(2,1)}, u32[]{:S(2)}) %copy-start.1) | copy-done | bytes 131096
  2.6 0.0 copy-start.3
  2.6 27.7 %analysis.1.ext_ref = f32[12,3,16,128]{3,2,1,0:T(8,128)S(1)} custom-call(bf16[64,2304]{1,0:T(8,128)(2,1)S(1)} %bitcast.4, bf16[64,1024]{1,0:T(8,128)(2,1)S(1)} %bitcast.5, s32[1,1024]{1,0:T(1,128)S(1)} %bitcast.6), custom_call_target="tpu_custom_call" | custom-call | tf_op jit(solution)/shard_map/analysis/pallas_call | solution.py:252
  30.2 0.0 copy-done.3
  30.2 1.8 %forecast.1 = f32[3,6,16,128]{3,2,1,0:T(8,128)} custom-call(f32[1,48]{1,0:T(1,128)S(1)} %copy-done.3, f32[12,3,16,128]{3,2,1,0:T(8,128)S(1)} %analysis.1.ext_ref), custom_call_target="tpu_custom_call" | custom-call | tf_op jit(solution)/shard_map/forecast/pallas_call | solution.py:284
Async XLA Ops:
  0.0 0.7 %copy-start.2 = (s32[1024]{0:T(1024)S(1)}, s32[1024]{0:T(1024)}, u32[]{:S(2)}) copy-start(s32[1024]{0:T(1024)} %param.6) | copy-start | bytes 12292
  0.7 1.0 %copy-start = (bf16[2304,64]{0,1:T(8,128)(2,1)S(1)}, bf16[2304,64]{0,1:T(8,128)(2,1)}, u32[]{:S(2)}) copy-start(bf16[2304,64]{0,1:T(8,128)(2,1)} %param.4) | copy-start | bytes 884740
  1.6 0.9 %copy-start.1 = (bf16[1024,64]{0,1:T(8,128)(2,1)S(1)}, bf16[1024,64]{0,1:T(8,128)(2,1)}, u32[]{:S(2)}) copy-start(bf16[1024,64]{0,1:T(8,128)(2,1)} %param.5) | copy-start | bytes 393220
  2.6 27.7 %copy-start.3 = (f32[1,48]{1,0:T(1,128)S(1)}, f32[1,48]{1,0:T(1,128)}, u32[]{:S(2)}) copy-start(f32[1,48]{1,0:T(1,128)} %constant.2.clone.coriolis_ref) | copy-start | bytes 580

commit v3 on v2

--- a/solution.py
+++ b/solution.py
@@ -2,7 +2,6 @@
 
 import jax
 import jax.numpy as jnp
-import numpy as np
 from jax import lax
 from jax.experimental import pallas as pl
 from jax.experimental.pallas import tpu as pltpu
@@ -25,8 +24,8 @@
 
 def analysis_kernel(
     n_st, n_ob, ens_hbm, w_hbm, col_hbm, out_ref, ens_ref, w_ref, col_ref, loaded,
-    anom_t, anom, w, picked, part, gathered, obs_t, taper, inc, inc_send, inc_recv,
-    p_send, p_recv, g_send, g_recv, i_send, i_recv, h_send, h_recv,
+    anom_t, anom, w, picked, part, gathered, obs_t, taper, acc, inc, inc_send, inc_recv,
+    ext, halo_send, halo_recv, turn, p_send, p_recv, g_send, g_recv, i_send, i_recv, h_send, h_recv,
 ):
     st, ob = lax.axis_index("st"), lax.axis_index("ob")
     members, rows = ens_ref.shape
@@ -35,6 +34,9 @@
     lats = rows // (FIELDS * NLON)
     blocks = rows // NLON
     chunk = obs // n_st
+    groups = obs_t.shape[0]
+    width = obs // groups
+    chunks = n_st // groups
     radius2 = float((lats * n_st) ** 2)
 
     loads = [
@@ -84,7 +86,8 @@
     loads[2].wait()
     for b in range(obs // NLON):
         at = slice(b * NLON, (b + 1) * NLON)
-        w[at, :] = w_ref[:, at].astype(F32).T.astype(BF16)
+        g, i = divmod(b * NLON, width)
+        w[g, i:i + NLON, :] = w_ref[:, at].astype(F32).T.astype(BF16)
     obs_lat = jnp.floor((column.astype(F32) + 0.5) * (1.0 / (FIELDS * NLON)))
     obs_lon = (column & (NLON - 1)).astype(F32)
     lon = lax.broadcasted_iota(jnp.int32, (NLON, obs), 0).astype(F32)
@@ -95,7 +98,12 @@
     for l in range(lats):
         lat_gap = obs_lat - (st * lats + l).astype(F32)
         fall = jnp.maximum(lon_left - lat_gap * lat_gap, 0.0)
-        taper[l] = fall * (fall * scale)
+        fall = fall * (fall * scale)
+        for g in range(groups):
+            taper[g, l] = fall[:, g * width:(g + 1) * width]
+    latitude = lax.broadcasted_iota(jnp.int32, turn.shape, 0) + (st * lats - STEPS)
+    angle = (latitude.astype(F32) + 0.5) / (lats * n_st) - 0.5
+    turn[...] = 0.8 * jnp.sin(jnp.pi * angle)
 
     for copy in first:
         copy.wait_recv()
@@ -107,15 +115,44 @@
     second = []
     for d in range(1, n_st):
         peer = lax.rem(st + d, n_st)
-        second.append(remote(gathered.at[st], gathered.at[st], g_send.at[d], g_recv.at[d], {"st": peer}))
+        second.append(remote(gathered.at[st], gathered.at[st], g_send.at[d], g_recv.at[st], {"st": peer}))
     for copy in second:
         copy.start()
-    for copy in second:
-        copy.wait_recv()
-    for c in range(n_st):
-        obs_t[:, c * chunk:(c + 1) * chunk] = gathered[c]
-
-    width = min(256, obs)
+
+    home = st // chunks
+
+    def arrive(q):
+        group = lax.rem(home + q, groups)
+        for i in range(chunks):
+            source = group * chunks + i
+
+            @pl.when(source != st)
+            def _():
+                here = gathered.at[source]
+                remote(here, here, g_send.at[0], g_recv.at[source], {"st": source}).wait_recv()
+
+            obs_t[q, :, i * chunk:(i + 1) * chunk] = gathered[source]
+        return group
+
+    def product(q, group, l):
+        cov = jnp.dot(anom[l], obs_t[q], preferred_element_type=F32)
+        gain = cov.reshape(FIELDS, NLON, width) * taper[group, l][None]
+        gain = gain.astype(BF16).reshape(FIELDS * NLON, width)
+        return jnp.dot(gain, w[group], preferred_element_type=F32)
+
+    together = 3 if lats % 3 == 0 else 1
+    for q in range(groups - 1):
+        group = arrive(q)
+
+        def some(i, carry):
+            for j in range(together):
+                l = i * together + j
+                value = product(q, group, l)
+                acc[l] = value if q == 0 else acc[l] + value
+            return carry
+
+        lax.fori_loop(0, lats // together, some, 0)
+    last = arrive(groups - 1)
 
     def sends(l):
         return [
@@ -126,15 +163,8 @@
             for d in range(1, n_ob)
         ]
 
-    def latitude(l, carry):
-        total = jnp.zeros((FIELDS * NLON, members), F32)
-        a = anom[l]
-        for k in range(obs // width):
-            at = slice(k * width, (k + 1) * width)
-            cov = jnp.dot(a, obs_t[:, at], preferred_element_type=F32)
-            gain = cov.reshape(FIELDS, NLON, width) * taper[l, :, at][None]
-            gain = gain.astype(BF16).reshape(FIELDS * NLON, width)
-            total = total + jnp.dot(gain, w[at, :], preferred_element_type=F32)
+    def finish(l, carry):
+        total = acc[l] + product(groups - 1, last, l)
         for f in range(FIELDS):
             turned = total[f * NLON:(f + 1) * NLON, :].T.reshape(n_ob, per, NLON)
             inc[:, l, f] = turned
@@ -143,7 +173,7 @@
             copy.start()
         return carry
 
-    lax.fori_loop(0, lats, latitude, 0)
+    lax.fori_loop(0, lats, finish, 0)
 
     own = ens_ref[pl.ds(pl.multiple_of(ob * per, per), per), :].astype(F32)
     for l in range(lats):
@@ -153,16 +183,14 @@
             value = own[:, (l * FIELDS + f) * NLON:(l * FIELDS + f + 1) * NLON] + inc[ob, l, f]
             for d in range(1, n_ob):
                 value = value + inc_recv[d, l, f].astype(F32)
-            out_ref[STEPS + l, f] = value
-
-    up = remote(
-        out_ref.at[pl.ds(lats, STEPS)], out_ref.at[pl.ds(0, STEPS)],
-        h_send.at[0], h_recv.at[0], {"st": lax.rem(st + 1, n_st)},
+            ext[STEPS + l, f] = value
+
+    halo_send[0] = ext[lats:lats + STEPS].astype(BF16)
+    halo_send[1] = ext[STEPS:2 * STEPS].astype(BF16)
+    up = remote(halo_send.at[0], halo_recv.at[0], h_send.at[0], h_recv.at[0], {"st": lax.rem(st + 1, n_st)})
+    down = remote(
+        halo_send.at[1], halo_recv.at[1], h_send.at[1], h_recv.at[1], {"st": lax.rem(st + n_st - 1, n_st)}
     )
-    down = remote(
-        out_ref.at[pl.ds(STEPS, STEPS)], out_ref.at[pl.ds(STEPS + lats, STEPS)],
-        h_send.at[1], h_recv.at[1], {"st": lax.rem(st + n_st - 1, n_st)},
-    )
 
     @pl.when(st < n_st - 1)
     def _():
@@ -171,44 +199,45 @@
     @pl.when(st > 0)
     def _():
         down.start()
-
-    @pl.when(st == 0)
-    def _():
-        out_ref[0:STEPS] = jnp.zeros((STEPS,) + out_ref.shape[1:], F32)
-
-    @pl.when(st == n_st - 1)
-    def _():
-        out_ref[STEPS + lats:] = jnp.zeros((STEPS,) + out_ref.shape[1:], F32)
 
     for copy in first + second:
         copy.wait_send()
     for l in range(lats):
         for copy in sends(l):
             copy.wait_send()
+    edge = jnp.zeros((STEPS,) + ext.shape[1:], F32)
+
+    @pl.when(st == 0)
+    def _():
+        ext[0:STEPS] = edge
+
+    @pl.when(st == n_st - 1)
+    def _():
+        ext[STEPS + lats:] = edge
 
     @pl.when(st < n_st - 1)
     def _():
         up.wait_send()
         down.wait_recv()
+        ext[STEPS + lats:] = halo_recv[1].astype(F32)
 
     @pl.when(st > 0)
     def _():
         down.wait_send()
         up.wait_recv()
-
-
-def forecast_kernel(n_st, coriolis_ref, ext_ref, out_ref):
-    st = lax.axis_index("st")
-    lats = ext_ref.shape[0] - 2 * STEPS
-    lat_count = lats * n_st
-
+        ext[0:STEPS] = halo_recv[0].astype(F32)
+
+    forecast(st, lats, lats * n_st, ext, turn, out_ref)
+
+
+def forecast(st, lats, lat_count, ext, turn, out_ref):
     def east(q):
         return pltpu.roll(q, NLON - 1, 2)
 
     def west(q):
         return pltpu.roll(q, 1, 2)
 
-    h, u, v = (ext_ref[:, f] for f in range(FIELDS))
+    h, u, v = (ext[:, f] for f in range(FIELDS))
     for step in range(STEPS):
         flux_east = (1.0 + h[1:-1]) * u[1:-1]
         flux_north = (1.0 + h) * v
@@ -228,9 +257,9 @@
             latitude = base + i
             inside = (latitude >= 0) & (latitude < lat_count)
             keep = jnp.where(inside, F32(1.0), F32(0.0))
-            turn = coriolis_ref[0, jnp.clip(latitude, 0, lat_count - 1)]
-            tend_u = cu[i] * dlon[1][i] + cv[i] * dlat[1][i] + dlon[0][i] - turn * cv[i]
-            tend_v = cu[i] * dlon[2][i] + cv[i] * dlat[2][i] + dlat[0][i] + turn * cu[i]
+            force = turn[step + 1 + i:step + 2 + i, :]
+            tend_u = cu[i] * dlon[1][i] + cv[i] * dlat[1][i] + dlon[0][i] - force * cv[i]
+            tend_v = cu[i] * dlon[2][i] + cv[i] * dlat[2][i] + dlat[0][i] + force * cu[i]
             for f, tend in enumerate((divergence[i], tend_u, tend_v)):
                 value = around[f][i] - time_step * tend
                 if step < STEPS - 1:
@@ -247,11 +276,12 @@
     per = members // n_ob
     lats = rows // (FIELDS * NLON)
     chunk = obs // n_st
+    groups = 4 if n_st % 4 == 0 and obs % (4 * NLON) == 0 else 1
     vmem = pl.BlockSpec(memory_space=pltpu.VMEM)
     dma = pltpu.SemaphoreType.DMA
-    ext = pl.pallas_call(
+    fields = pl.pallas_call(
         functools.partial(analysis_kernel, n_st, n_ob),
-        out_shape=jax.ShapeDtypeStruct((lats + 2 * STEPS, FIELDS, per, NLON), F32),
+        out_shape=jax.ShapeDtypeStruct((FIELDS, lats, per, NLON), F32),
         in_specs=[pl.BlockSpec(memory_space=pltpu.HBM)] * 3,
         out_specs=vmem,
         scratch_shapes=[
@@ -261,15 +291,20 @@
             dma((3,)),
             pltpu.VMEM((members, rows), BF16),
             pltpu.VMEM((lats, FIELDS * NLON, members), BF16),
-            pltpu.VMEM((obs, members), BF16),
+            pltpu.VMEM((groups, obs // groups, members), BF16),
             pltpu.VMEM((n_st, members, chunk), BF16),
             pltpu.VMEM((n_st, members, chunk), BF16),
             pltpu.VMEM((n_st, members, chunk), BF16),
-            pltpu.VMEM((members, obs), BF16),
-            pltpu.VMEM((lats, NLON, obs), F32),
+            pltpu.VMEM((groups, members, obs // groups), BF16),
+            pltpu.VMEM((groups, lats, NLON, obs // groups), F32),
+            pltpu.VMEM((lats, FIELDS * NLON, members), F32),
             pltpu.VMEM((n_ob, lats, FIELDS, per, NLON), F32),
             pltpu.VMEM((n_ob, lats, FIELDS, per, NLON), BF16),
             pltpu.VMEM((n_ob, lats, FIELDS, per, NLON), BF16),
+            pltpu.VMEM((lats + 2 * STEPS, FIELDS, per, NLON), F32),
+            pltpu.VMEM((2, STEPS, FIELDS, per, NLON), BF16),
+            pltpu.VMEM((2, STEPS, FIELDS, per, NLON), BF16),
+            pltpu.VMEM((-(lats + 2 * STEPS) // 8 * -8, NLON), F32),
             dma((n_st,)), dma((n_st,)), dma((n_st,)), dma((n_st,)),
             dma((n_ob, lats)), dma((n_ob, lats)), dma((2,)), dma((2,)),
         ],
@@ -277,18 +312,7 @@
             collective_id=0, has_side_effects=True, vmem_limit_bytes=48 * 1024 * 1024
         ),
         name="analysis",
-    )(ensemble.T, weights.T, obs_column.reshape(1, obs))
-    lat_count = lats * n_st
-    degrees = (np.arange(lat_count, dtype=np.float32) + 0.5) / lat_count - 0.5
-    coriolis = (0.8 * np.sin(np.pi * degrees)).astype(np.float32).reshape(1, lat_count)
-    fields = pl.pallas_call(
-        functools.partial(forecast_kernel, n_st),
-        out_shape=jax.ShapeDtypeStruct((FIELDS, lats, per, NLON), F32),
-        in_specs=[pl.BlockSpec(memory_space=pltpu.SMEM), vmem],
-        out_specs=vmem,
-        compiler_params=pltpu.CompilerParams(vmem_limit_bytes=8 * 1024 * 1024),
-        name="forecast",
-    )(jnp.asarray(coriolis), ext)
+    )(*(pltpu.with_memory_space_constraint(x, pltpu.HBM) for x in (ensemble.T, weights.T, obs_column.reshape(1, obs))))
     return fields.transpose(2, 0, 1, 3)
 
 

time: 32.3 us -> 27.2 us (0.84)
  Pallas kernels: 29.5 us -> 26.4 us
  local copies, waits for them, and re-layouts: 2.55 us -> 0.66 us
    unnamed x8 -> x1, local copies, waits for them, and re-layouts: 2.55 us -> 0.66 us
    pallas_call x1 -> x0, Pallas kernels: 1.84 us -> none  [local(): pl.pallas_call(functools.partial(forecast_kernel, n_st), out_shape=jax.Sh...]
    pallas_call x1, Pallas kernels: 27.7 us -> 26.4 us  [local(): pl.pallas_call(functools.partial(analysis_kernel, n_st, n_ob), out_shape=...]
where the time goes in v3:
time: 27.2 us; the launch traced here: 27.1 us
  Pallas kernels  26.4 us (97%)
  local copies, waits for them, and re-layouts  0.66 us (2%)
    pallas_call x1, Pallas kernels, local(): pl.pallas_call(functools.partial(analysis_kernel, n_st, n_ob), out_shape=...  26.4 us
    unnamed x1, local copies, waits for them, and re-layouts  0.66 us

profile of v3, /device:TPU:0, one launch (start us, length us, event | category | flops | bytes accessed | tf_op | source)
XLA Modules:
  0.0 27.1 jit_solution(11299949971100125029)
XLA Ops:
  0.0 26.4 %analysis.1 = f32[3,6,16,128]{3,2,1,0:T(8,128)S(1)} custom-call(bf16[64,2304]{1,0:T(8,128)(2,1)} %bitcast.5, bf16[64,1024]{1,0:T(8,128)(2,1)} %bitcast.6, s32[1,1024]{1,0:T(1,128)} %bitcast.7), custom_call_target="tpu_custom_call" | custom-call | tf_op jit(solution)/shard_map/analysis/pallas_call | solution.py:282
  26.4 0.7 %copy.5 = f32[16,3,6,128]{3,0,2,1:T(8,128)} copy(f32[16,3,6,128]{3,0,2,1:T(8,128)S(1)} %bitcast.4) | data formatting | bytes 294912
